TPU v7x, 32 devices: a whole 2x2x4 slice. The times are simulated.
32 devices in a mesh: dp: 4 (over z), fsdp: 8 (over y, x, core).
Axes of the slice: x: 2, y: 2, z: 4, core: 2. Of those that a mesh axis runs over, the one named last changes fastest.
Arguments:
- tokens: bfloat16 [4096, 1280], P(('dp', 'fsdp')), may hold values from -6 to 6
- lengths: int32 [32, 2], P(('dp', 'fsdp')), may hold values from 1 to 96, 128 in all within a row
- padding: int32 [4096], P(('dp', 'fsdp')), may hold values 0 or 1
- ln1_gain: bfloat16 [1280], P('fsdp'), may hold values from 0.099609375 to 1.8984375
- ln1_bias: bfloat16 [1280], P('fsdp'), may hold values from -4 to 4
- w_qkv: bfloat16 [1280, 3840], P('fsdp'), may hold values from -0.15625 to 0.15625
- b_query: bfloat16 [1280], P('fsdp'), may hold values from -4 to 4
- b_value: bfloat16 [1280], P('fsdp'), may hold values from -4 to 4
- w_out: bfloat16 [1280, 1280], P('fsdp'), may hold values from -0.625 to 0.625
- b_out: bfloat16 [1280], P('fsdp'), may hold values from -4 to 4
- ln2_gain: bfloat16 [1280], P('fsdp'), may hold values from 0.099609375 to 1.8984375
- ln2_bias: bfloat16 [1280], P('fsdp'), may hold values from -4 to 4
- w_up: bfloat16 [1280, 5120], P('fsdp'), may hold values from -0.15625 to 0.15625
- b_up: bfloat16 [5120], P('fsdp'), may hold values from -6 to 6
- w_down: bfloat16 [5120, 1280], P('fsdp'), may hold values from -0.078125 to 0.078125
- b_down: bfloat16 [1280], P('fsdp'), may hold values from -4 to 4
- cotangent: bfloat16 [4096, 1280], P(('dp', 'fsdp')), may hold values from -6 to 6
Outputs:
- layer_out: bfloat16 [4096, 1280], P(('dp', 'fsdp'))
- grad_tokens: float32 [4096, 1280], P(('dp', 'fsdp'))
- grad_ln1_gain: float32 [1280], P('fsdp')
- grad_ln1_bias: float32 [1280], P('fsdp')
- grad_w_qkv: float32 [1280, 3840], P('fsdp')
- grad_b_query: float32 [1280], P('fsdp')
- grad_b_value: float32 [1280], P('fsdp')
- grad_w_out: float32 [1280, 1280], P('fsdp')
- grad_b_out: float32 [1280], P('fsdp')
- grad_ln2_gain: float32 [1280], P('fsdp')
- grad_ln2_bias: float32 [1280], P('fsdp')
- grad_w_up: float32 [1280, 5120], P('fsdp')
- grad_b_up: float32 [5120], P('fsdp')
- grad_w_down: float32 [5120, 1280], P('fsdp')
- grad_b_down: float32 [1280], P('fsdp')
- cls_mean: float32 [1280], replicated
- cls_var: float32 [1280], replicated
Inputs may be any that keep to these rules, and one draw needn't show every extreme that they name: `lengths`: each row sums to 128; each length lies between 32 and 96. `padding`: A CLS token is a key whatever its mark.
All inputs are finite; a program needn't handle non-finite values. No bound on the sum of `padding` on one device may be relied on, other than what follows from the above.
Results may differ from a plain program's by a relative error of at most 0.015.
Values may be sent and summed in bfloat16 or wider, within the bound.
No kernel may reach another device: no remote copies, remote signals or barrier semaphores. Data moves between devices by JAX's collectives and lax.ppermute only.
A program may use at most 256 MiB of HBM per device.

v0:
```python
from functools import partial
import jax
import jax.numpy as jnp
from jax import lax
from jax.sharding import PartitionSpec as P

D = 1280
HEADS = 20
HEAD_DIM = 64
CELLS_DEV = 2
EPS = 1e-05


def norm_forward(values, norm_gain, norm_bias):
    center = jnp.mean(values, axis=-1, keepdims=True)
    centred = values - center
    spread = jnp.mean(centred * centred, axis=-1, keepdims=True)
    inverse = lax.rsqrt(spread + EPS)
    normed = centred * inverse
    return (normed * norm_gain + norm_bias, normed, inverse)


def norm_backward(grad_out, normed, inverse, norm_gain):
    grad_normed = grad_out * norm_gain
    first_mean = jnp.mean(grad_normed, axis=-1, keepdims=True)
    second_mean = jnp.mean(grad_normed * normed, axis=-1, keepdims=True)
    grad_in = inverse * (grad_normed - first_mean - normed * second_mean)
    return (grad_in, jnp.sum(grad_out * normed, axis=0), jnp.sum(grad_out, axis=0))


def cell_layout(lengths_row, padding_row):
    places = jnp.arange(padding_row.shape[0], dtype=jnp.int32)
    finish = jnp.cumsum(lengths_row)
    starts = finish - lengths_row
    member = jnp.sum((places[:, None] >= finish[None, :]).astype(jnp.int32), axis=1)
    leading = jnp.any(places[:, None] == starts[None, :], axis=1)
    usable = (padding_row > 0) | leading
    allowed = (member[:, None] == member[None, :]) & usable[None, :]
    return (allowed, leading)


def masked_scores(query_low, key_low, allowed, score_scale):
    raw = jnp.einsum("thd,shd->hts", query_low, key_low, preferred_element_type=jnp.float32)
    return jnp.where(allowed[None], raw * score_scale, -1e30)


def reduce_late(values):
    owned = (
        lax.psum_scatter(values[0], "fsdp", scatter_dimension=0, tiled=True),
        lax.psum_scatter(values[1], "fsdp", scatter_dimension=0, tiled=True),
        lax.psum_scatter(values[2], "fsdp", scatter_dimension=0, tiled=True),
        lax.psum_scatter(values[3], "fsdp", scatter_dimension=0, tiled=True),
        lax.psum_scatter(values[4], "fsdp", scatter_dimension=0, tiled=True),
        lax.psum_scatter(values[5], "fsdp", scatter_dimension=0, tiled=True),
        lax.psum_scatter(values[6], "fsdp", scatter_dimension=0, tiled=True),
        lax.psum_scatter(values[7], "fsdp", scatter_dimension=0, tiled=True),
        lax.psum_scatter(values[8], "fsdp", scatter_dimension=0, tiled=True),
        lax.psum_scatter(values[9], "fsdp", scatter_dimension=0, tiled=True),
        lax.psum_scatter(values[10], "fsdp", scatter_dimension=0, tiled=True),
        lax.psum_scatter(values[11], "fsdp", scatter_dimension=0, tiled=True),
        lax.psum_scatter(values[12], "fsdp", scatter_dimension=0, tiled=True),
    )
    shares = (
        lax.psum_scatter(
            owned[0].astype(jnp.bfloat16), "dp", scatter_dimension=0, tiled=True
        ).astype(jnp.float32),
        lax.psum_scatter(
            owned[1].astype(jnp.bfloat16), "dp", scatter_dimension=0, tiled=True
        ).astype(jnp.float32),
        lax.psum_scatter(
            owned[2].astype(jnp.bfloat16), "dp", scatter_dimension=0, tiled=True
        ).astype(jnp.float32),
        lax.psum_scatter(
            owned[3].astype(jnp.bfloat16), "dp", scatter_dimension=0, tiled=True
        ).astype(jnp.float32),
        lax.psum_scatter(
            owned[4].astype(jnp.bfloat16), "dp", scatter_dimension=0, tiled=True
        ).astype(jnp.float32),
        lax.psum_scatter(
            owned[5].astype(jnp.bfloat16), "dp", scatter_dimension=0, tiled=True
        ).astype(jnp.float32),
        lax.psum_scatter(
            owned[6].astype(jnp.bfloat16), "dp", scatter_dimension=0, tiled=True
        ).astype(jnp.float32),
        lax.psum_scatter(
            owned[7].astype(jnp.bfloat16), "dp", scatter_dimension=0, tiled=True
        ).astype(jnp.float32),
        lax.psum_scatter(
            owned[8].astype(jnp.bfloat16), "dp", scatter_dimension=0, tiled=True
        ).astype(jnp.float32),
        lax.psum_scatter(
            owned[9].astype(jnp.bfloat16), "dp", scatter_dimension=0, tiled=True
        ).astype(jnp.float32),
        lax.psum_scatter(
            owned[10].astype(jnp.bfloat16), "dp", scatter_dimension=0, tiled=True
        ).astype(jnp.float32),
        lax.psum_scatter(
            owned[11].astype(jnp.bfloat16), "dp", scatter_dimension=0, tiled=True
        ).astype(jnp.float32),
        lax.psum_scatter(
            owned[12].astype(jnp.bfloat16), "dp", scatter_dimension=0, tiled=True
        ).astype(jnp.float32),
    )
    return (
        lax.all_gather(shares[0].astype(jnp.bfloat16), "dp", axis=0, tiled=True).astype(
            jnp.float32
        ),
        lax.all_gather(shares[1].astype(jnp.bfloat16), "dp", axis=0, tiled=True).astype(
            jnp.float32
        ),
        lax.all_gather(shares[2].astype(jnp.bfloat16), "dp", axis=0, tiled=True).astype(
            jnp.float32
        ),
        lax.all_gather(shares[3].astype(jnp.bfloat16), "dp", axis=0, tiled=True).astype(
            jnp.float32
        ),
        lax.all_gather(shares[4].astype(jnp.bfloat16), "dp", axis=0, tiled=True).astype(
            jnp.float32
        ),
        lax.all_gather(shares[5].astype(jnp.bfloat16), "dp", axis=0, tiled=True).astype(
            jnp.float32
        ),
        lax.all_gather(shares[6].astype(jnp.bfloat16), "dp", axis=0, tiled=True).astype(
            jnp.float32
        ),
        lax.all_gather(shares[7].astype(jnp.bfloat16), "dp", axis=0, tiled=True).astype(
            jnp.float32
        ),
        lax.all_gather(shares[8].astype(jnp.bfloat16), "dp", axis=0, tiled=True).astype(
            jnp.float32
        ),
        lax.all_gather(shares[9].astype(jnp.bfloat16), "dp", axis=0, tiled=True).astype(
            jnp.float32
        ),
        lax.all_gather(shares[10].astype(jnp.bfloat16), "dp", axis=0, tiled=True).astype(
            jnp.float32
        ),
        lax.all_gather(shares[11].astype(jnp.bfloat16), "dp", axis=0, tiled=True).astype(
            jnp.float32
        ),
        lax.all_gather(shares[12].astype(jnp.bfloat16), "dp", axis=0, tiled=True).astype(
            jnp.float32
        ),
    )


def local(
    tokens,
    lengths,
    padding,
    ln1_gain,
    ln1_bias,
    w_qkv,
    b_query,
    b_value,
    w_out,
    b_out,
    ln2_gain,
    ln2_bias,
    w_up,
    b_up,
    w_down,
    b_down,
    cotangent,
):
    fsdp_count = lax.axis_size("fsdp")
    dp_count = lax.axis_size("dp")
    f32 = jnp.float32
    bf16 = jnp.bfloat16
    row_total = tokens.shape[0]
    score_scale = HEAD_DIM ** (-0.5)
    (
        first_gain,
        first_bias,
        whole_qkv,
        query_bias,
        value_bias,
        whole_out,
        out_bias,
        second_gain,
        second_bias,
        whole_up,
        up_bias,
        whole_down,
        down_bias,
    ) = (
        lax.all_gather(ln1_gain, "fsdp", axis=0, tiled=True),
        lax.all_gather(ln1_bias, "fsdp", axis=0, tiled=True),
        lax.all_gather(w_qkv, "fsdp", axis=0, tiled=True),
        lax.all_gather(b_query, "fsdp", axis=0, tiled=True),
        lax.all_gather(b_value, "fsdp", axis=0, tiled=True),
        lax.all_gather(w_out, "fsdp", axis=0, tiled=True),
        lax.all_gather(b_out, "fsdp", axis=0, tiled=True),
        lax.all_gather(ln2_gain, "fsdp", axis=0, tiled=True),
        lax.all_gather(ln2_bias, "fsdp", axis=0, tiled=True),
        lax.all_gather(w_up, "fsdp", axis=0, tiled=True),
        lax.all_gather(b_up, "fsdp", axis=0, tiled=True),
        lax.all_gather(w_down, "fsdp", axis=0, tiled=True),
        lax.all_gather(b_down, "fsdp", axis=0, tiled=True),
    )
    allowed, leading = cell_layout(lengths[0], padding)
    inputs = tokens.astype(f32)
    first_out, first_normed, first_inverse = norm_forward(
        inputs, first_gain.astype(f32), first_bias.astype(f32)
    )
    first_low = first_out.astype(bf16)
    projected = jnp.dot(first_low, whole_qkv, preferred_element_type=f32)
    query_low = (
        (projected[:, :D] + query_bias.astype(f32)).astype(bf16).reshape(row_total, HEADS, HEAD_DIM)
    )
    key_low = projected[:, D : 2 * D].astype(bf16).reshape(row_total, HEADS, HEAD_DIM)
    value_low = (
        (projected[:, 2 * D :] + value_bias.astype(f32))
        .astype(bf16)
        .reshape(row_total, HEADS, HEAD_DIM)
    )
    masked = masked_scores(query_low, key_low, allowed, score_scale)
    top_score = jnp.max(masked, axis=-1, keepdims=True)
    log_total = top_score + jnp.log(jnp.sum(jnp.exp(masked - top_score), axis=-1, keepdims=True))
    probs_low = jnp.exp(masked - log_total).astype(bf16)
    context = jnp.einsum("hts,shd->thd", probs_low, value_low, preferred_element_type=f32)
    context_low = context.reshape(row_total, D).astype(bf16)
    mixed = (
        inputs + jnp.dot(context_low, whole_out, preferred_element_type=f32) + out_bias.astype(f32)
    )
    second_out, second_normed, second_inverse = norm_forward(
        mixed, second_gain.astype(f32), second_bias.astype(f32)
    )
    second_low = second_out.astype(bf16)
    hidden_pre = jnp.dot(second_low, whole_up, preferred_element_type=f32) + up_bias.astype(f32)
    activated, gelu_pull = jax.vjp(partial(jax.nn.gelu, approximate=False), hidden_pre)
    act_low = activated.astype(bf16)
    result = (
        mixed + jnp.dot(act_low, whole_down, preferred_element_type=f32) + down_bias.astype(f32)
    )
    picked = jnp.where(leading[:, None], result, 0.0)
    moment_sum, moment_square = lax.psum(
        (jnp.sum(picked, axis=0), jnp.sum(picked * picked, axis=0)), ("dp", "fsdp")
    )
    cell_total = CELLS_DEV * dp_count * fsdp_count
    cls_mean = moment_sum / cell_total
    cls_var = moment_square / cell_total - cls_mean * cls_mean
    (
        first_gain,
        first_bias,
        whole_qkv,
        query_bias,
        value_bias,
        whole_out,
        out_bias,
        second_gain,
        second_bias,
        whole_up,
        up_bias,
        whole_down,
        down_bias,
    ) = (
        lax.all_gather(ln1_gain, "fsdp", axis=0, tiled=True),
        lax.all_gather(ln1_bias, "fsdp", axis=0, tiled=True),
        lax.all_gather(w_qkv, "fsdp", axis=0, tiled=True),
        lax.all_gather(b_query, "fsdp", axis=0, tiled=True),
        lax.all_gather(b_value, "fsdp", axis=0, tiled=True),
        lax.all_gather(w_out, "fsdp", axis=0, tiled=True),
        lax.all_gather(b_out, "fsdp", axis=0, tiled=True),
        lax.all_gather(ln2_gain, "fsdp", axis=0, tiled=True),
        lax.all_gather(ln2_bias, "fsdp", axis=0, tiled=True),
        lax.all_gather(w_up, "fsdp", axis=0, tiled=True),
        lax.all_gather(b_up, "fsdp", axis=0, tiled=True),
        lax.all_gather(w_down, "fsdp", axis=0, tiled=True),
        lax.all_gather(b_down, "fsdp", axis=0, tiled=True),
    )
    grad_result = cotangent.astype(f32)
    grad_down_bias = jnp.sum(grad_result, axis=0)
    grad_whole_down = jnp.einsum("tf,td->fd", act_low, cotangent, preferred_element_type=f32)
    grad_act = jnp.einsum("td,fd->tf", cotangent, whole_down, preferred_element_type=f32)
    grad_pre = gelu_pull(grad_act)[0].astype(bf16)
    grad_up_bias = jnp.sum(grad_pre.astype(f32), axis=0)
    grad_whole_up = jnp.einsum("td,tf->df", second_low, grad_pre, preferred_element_type=f32)
    grad_second = jnp.einsum("tf,df->td", grad_pre, whole_up, preferred_element_type=f32)
    grad_from_second, grad_second_gain, grad_second_bias = norm_backward(
        grad_second, second_normed, second_inverse, second_gain.astype(f32)
    )
    grad_mixed = grad_result + grad_from_second
    grad_branch = grad_mixed.astype(bf16)
    grad_out_bias = jnp.sum(grad_branch.astype(f32), axis=0)
    grad_whole_out = jnp.einsum("td,te->de", context_low, grad_branch, preferred_element_type=f32)
    grad_context = jnp.einsum("te,de->td", grad_branch, whole_out, preferred_element_type=f32)
    grad_context = grad_context.astype(bf16).reshape(row_total, HEADS, HEAD_DIM)
    masked = masked_scores(query_low, key_low, allowed, score_scale)
    probs = jnp.exp(masked - log_total)
    probs_low = probs.astype(bf16)
    grad_probs = jnp.einsum("thd,shd->hts", grad_context, value_low, preferred_element_type=f32)
    along = jnp.sum(grad_probs * probs, axis=-1, keepdims=True)
    grad_scores = (probs * (grad_probs - along) * score_scale).astype(bf16)
    grad_value = jnp.einsum(
        "hts,thd->shd", probs_low, grad_context, preferred_element_type=f32
    ).astype(bf16)
    grad_query = jnp.einsum(
        "hts,shd->thd", grad_scores, key_low, preferred_element_type=f32
    ).astype(bf16)
    grad_key = jnp.einsum(
        "hts,thd->shd", grad_scores, query_low, preferred_element_type=f32
    ).astype(bf16)
    grad_query = grad_query.reshape(row_total, D)
    grad_key = grad_key.reshape(row_total, D)
    grad_value = grad_value.reshape(row_total, D)
    grad_query_bias = jnp.sum(grad_query.astype(f32), axis=0)
    grad_value_bias = jnp.sum(grad_value.astype(f32), axis=0)
    grad_projected = jnp.concatenate([grad_query, grad_key, grad_value], axis=1)
    grad_whole_qkv = jnp.einsum("td,te->de", first_low, grad_projected, preferred_element_type=f32)
    grad_first = jnp.einsum("te,de->td", grad_projected, whole_qkv, preferred_element_type=f32)
    grad_from_first, grad_first_gain, grad_first_bias = norm_backward(
        grad_first, first_normed, first_inverse, first_gain.astype(f32)
    )
    grad_inputs = grad_mixed + grad_from_first
    totals = reduce_late(
        (
            grad_first_gain,
            grad_first_bias,
            grad_whole_qkv,
            grad_query_bias,
            grad_value_bias,
            grad_whole_out,
            grad_out_bias,
            grad_second_gain,
            grad_second_bias,
            grad_whole_up,
            grad_up_bias,
            grad_whole_down,
            grad_down_bias,
        )
    )
    return (
        result.astype(bf16),
        grad_inputs,
        totals[0],
        totals[1],
        totals[2],
        totals[3],
        totals[4],
        totals[5],
        totals[6],
        totals[7],
        totals[8],
        totals[9],
        totals[10],
        totals[11],
        totals[12],
        cls_mean,
        cls_var,
    )


def solution(mesh):
    in_specs = (
        P(("dp", "fsdp"), None),
        P(("dp", "fsdp"), None),
        P(("dp", "fsdp")),
        P("fsdp"),
        P("fsdp"),
        P("fsdp", None),
        P("fsdp"),
        P("fsdp"),
        P("fsdp", None),
        P("fsdp"),
        P("fsdp"),
        P("fsdp"),
        P("fsdp", None),
        P("fsdp"),
        P("fsdp", None),
        P("fsdp"),
        P(("dp", "fsdp"), None),
    )
    out_specs = (
        P(("dp", "fsdp"), None),
        P(("dp", "fsdp"), None),
        P("fsdp"),
        P("fsdp"),
        P("fsdp", None),
        P("fsdp"),
        P("fsdp"),
        P("fsdp", None),
        P("fsdp"),
        P("fsdp"),
        P("fsdp"),
        P("fsdp", None),
        P("fsdp"),
        P("fsdp", None),
        P("fsdp"),
        P(),
        P(),
    )
    return jax.shard_map(local, mesh=mesh, in_specs=in_specs, out_specs=out_specs, check_vma=False)
```

profile of v0, /device:TPU:0, one launch (start us, length us, event | category | flops | bytes accessed | tf_op | source)
XLA Modules:
  0.0 1096.7 jit_solution(2530237779539740819)
XLA Ops:
  13.5 25.9 %all-reduce.37 = (bf16[1280]{0:T(1024)(128)(2,1)S(1)}, bf16[1280]{0:T(1024)(128)(2,1)S(1)}, bf16[1280]{0:T(1024)(128)(2,1)S(1)}, bf16[1280]{0:T(1024)(128)(2,1)S...) all-reduce(bf16[1280]{0:T(1024)(128)(2,1)S(1)} %dynamic-update-slic, ...), channel_id=1, replica_groups=mesh['dp'=4,'fsdp'=8] {'fsdp'}, use_global_device_ids=true, to_apply=%add.1 | all-reduce | flops 10240 | bytes 40960
  39.5 8.1 all-gather
  48.6 24.9 %all-gather.9.cloned.1.call-done = bf16[1280,3840]{1,0:T(8,128)(2,1)} async-done(((bf16[160,3840]{1,0:T(8,128)(2,1)}), bf16[1280,3840]{1,0:T(8,128)(2,1)}) %all-gather.9.cloned.1.call-update) | async-done | bytes 9830416 | tf_op jit(solution)/shard_map/all_gather | solution.py:189
  81.4 26.8 %all-gather.11.cloned.1.call-done = bf16[1280,1280]{1,0:T(8,128)(2,1)} async-done(((bf16[160,1280]{1,0:T(8,128)(2,1)}), bf16[1280,1280]{1,0:T(8,128)(2,1)}) %all-gather.11.cloned.1.call-update) | async-done | bytes 3276816 | tf_op jit(solution)/shard_map/all_gather | solution.py:192
  111.1 73.4 %all-gather.13.cloned.1.call-done = bf16[1280,5120]{1,0:T(8,128)(2,1)} async-done(((bf16[160,5120]{1,0:T(8,128)(2,1)}), bf16[1280,5120]{1,0:T(8,128)(2,1)}) %all-gather.13.cloned.1.call-update) | async-done | bytes 13107216 | tf_op jit(solution)/shard_map/all_gather | solution.py:196
  184.5 8.2 convolution_add_fusion
  192.7 67.9 %all-gather.15.cloned.1.call-done = bf16[5120,1280]{1,0:T(8,128)(2,1)} async-done(((bf16[640,1280]{1,0:T(8,128)(2,1)}), bf16[5120,1280]{1,0:T(8,128)(2,1)}) %all-gather.15.cloned.1.call-update) | async-done | bytes 13107216 | tf_op jit(solution)/shard_map/all_gather | solution.py:198
  260.6 14.4 %convert_reduce_fusion = (f32[5120]{0:T(1024)S(1)}, bf16[128,5120]{1,0:T(8,128)(2,1)}, f32[128,5120]{1,0:T(8,128)}) fusion(f32[128,5120]{1,0:T(8,128)} %convolution_add_fusion, bf16[128,1280]{1,0:T(8,128)(2,1)} %param.33, bf16[5120,1280]{1,0:T(8,128)(2,1)} %all-gather.15.cloned.1.call-done), kind=kOutput, calls=%fused_computation.4 | convolution fusion | flops 1726213120 | bytes 20008960 | tf_op jit(solution)/shard_map/td,fd->tf/dot_general | solution.py:275
  300.0 9.3 fusion.50
  310.6 15.4 %fusion.68 = f32[1280,5120]{1,0:T(8,128)} fusion(bf16[128,5120]{1,0:T(8,128)(2,1)S(1)} %copy-done.4, f32[128,1280]{1,0:T(8,128)S(1)} %get-tuple-element.82, f32[1280]{0:T(1024)S(1)} %convert_element_type.233, f32[1280]{0:T(1024)S(1)} %convert_element_type.232, f32[128]{0:T(128)S(1)} %add_rsqrt_fusion, f32[128]{0:T(128)S(1)} %broadcast_multiply_fusion.5), kind=kOutput, calls=%fused_computation.121 | convolution fusion | flops 1678540800 | bytes 28191744 | tf_op jit(solution)/shard_map/td,tf->df/dot_general | solution.py:278
  330.2 12.7 %fusion.77 = f32[5120,1280]{1,0:T(8,128)} fusion(bf16[128,5120]{1,0:T(8,128)(2,1)S(1)} %multiply_convert_fusion, bf16[128,1280]{1,0:T(8,128)(2,1)S(1)} %copy-done.8), kind=kOutput, calls=%fused_computation.127 | convolution fusion | flops 1677721600 | bytes 27852800 | tf_op jit(solution)/shard_map/tf,td->fd/dot_general | solution.py:274
  346.8 92.3 %reduce-scatter.9.cloned.1.call-done = f32[160,3840]{1,0:T(8,128)} async-done(((f32[1280,3840]{1,0:T(8,128)}), f32[160,3840]{1,0:T(8,128)}) %reduce-scatter.9.cloned.1.call-update) | async-done | bytes 2457616 | tf_op jit(solution)/shard_map/reduce_scatter | solution.py:51
  442.1 163.0 %reduce-scatter.17.cloned.1.call-done = f32[160,5120]{1,0:T(8,128)} async-done(((f32[1280,5120]{1,0:T(8,128)}), f32[160,5120]{1,0:T(8,128)}) %reduce-scatter.17.cloned.1.call-update) | async-done | bytes 3276816 | tf_op jit(solution)/shard_map/reduce_scatter | solution.py:58
  608.5 162.7 %reduce-scatter.21.cloned.1.call-done = f32[640,1280]{1,0:T(8,128)} async-done(((f32[5120,1280]{1,0:T(8,128)}), f32[640,1280]{1,0:T(8,128)}) %reduce-scatter.21.cloned.1.call-update) | async-done | bytes 3276816 | tf_op jit(solution)/shard_map/reduce_scatter | solution.py:60
  774.5 63.1 %reduce-scatter.13.cloned.1.call-done = f32[160,1280]{1,0:T(8,128)} async-done(((f32[1280,1280]{1,0:T(8,128)}), f32[160,1280]{1,0:T(8,128)}) %reduce-scatter.13.cloned.1.call-update) | async-done | bytes 819216 | tf_op jit(solution)/shard_map/reduce_scatter | solution.py:54
  839.6 31.1 %reduce-scatter.11.cloned.1.call-done = bf16[40,3840]{1,0:T(8,128)(2,1)} async-done(((bf16[160,3840]{1,0:T(8,128)(2,1)}), bf16[40,3840]{1,0:T(8,128)(2,1)}) %reduce-scatter.11.cloned.1.call-update) | async-done | bytes 307216 | tf_op jit(solution)/shard_map/reduce_scatter | solution.py:70
  870.8 37.8 %reduce-scatter.19.cloned.1.call-done = bf16[40,5120]{1,0:T(8,128)(2,1)} async-done(((bf16[160,5120]{1,0:T(8,128)(2,1)}), bf16[40,5120]{1,0:T(8,128)(2,1)}) %reduce-scatter.19.cloned.1.call-update) | async-done | bytes 409616 | tf_op jit(solution)/shard_map/reduce_scatter | solution.py:91
  912.6 34.4 %reduce-scatter.23.cloned.1.call-done = bf16[160,1280]{1,0:T(8,128)(2,1)} async-done(((bf16[640,1280]{1,0:T(8,128)(2,1)}), bf16[160,1280]{1,0:T(8,128)(2,1)}) %reduce-scatter.23.cloned.1.call-update) | async-done | bytes 409616 | tf_op jit(solution)/shard_map/reduce_scatter | solution.py:97
  947.0 8.2 fusion.40
  955.4 25.2 %all-reduce.36 = (bf16[1280]{0:T(1024)(128)(2,1)S(1)}, bf16[1280]{0:T(1024)(128)(2,1)S(1)}, bf16[1280]{0:T(1024)(128)(2,1)S(1)}, bf16[1280]{0:T(1024)(128)(2,1)S...) all-reduce(f32[1280]{0:T(1024)S(1)} %get-tuple-element.19, ...), channel_id=2, replica_groups=mesh['dp'=4,'fsdp'=8] {'fsdp'}, use_global_device_ids=true, to_apply=%region_15.16.clone | all-reduce | flops 15360 | bytes 92160
  981.3 10.8 all-reduce.39
  994.6 9.6 all-reduce.38
  1016.9 40.5 %all-reduce.35 = (f32[1280]{0:T(1024)S(1)}, f32[1280]{0:T(1024)S(1)}) all-reduce(f32[1280]{0:T(1024)S(1)} %get-tuple-element.24, f32[1280]{0:T(1024)S(1)} %get-tuple-element.23), channel_id=1, replica_groups=mesh['dp'=4,'fsdp'=8] {'dp','fsdp'}, use_global_device_ids=true, to_apply=%region_50.51 | all-reduce | flops 2560 | bytes 20480 | tf_op jit(solution)/shard_map/psum | solution.py:237
  1060.1 18.6 %all_gather.102 = bf16[160,1280]{1,0:T(8,128)(2,1)S(1)} all-gather(bf16[40,1280]{1,0:T(8,128)(2,1)} %reduce-scatter.15.cloned.1.call-done), channel_id=1, replica_groups=mesh['dp'=4,'fsdp'=8] {'dp'}, dimensions={0}, use_global_device_ids=true | all-gather | bytes 512000 | tf_op jit(solution)/shard_map/all_gather | solution.py:120
  (203 shorter events, 93.2 us)
Async XLA Ops:
  7.3 5.5 copy-start.18
  7.3 5.8 copy-start.19
  7.3 6.0 copy-start.20
  7.3 40.4 %copy-start.21 = (s32[1,2]{1,0:T(1,128)S(1)}, s32[1,2]{1,0:T(1,128)}, u32[]{:S(2)}) copy-start(s32[1,2]{1,0:T(1,128)} %param.18) | copy-start | bytes 28
  7.3 40.7 %copy-start.3 = (bf16[128,1280]{1,0:T(8,128)(2,1)S(1)}, bf16[128,1280]{1,0:T(8,128)(2,1)}, u32[]{:S(2)}) copy-start(bf16[128,1280]{1,0:T(8,128)(2,1)} %param.17) | copy-start | bytes 983044
  7.3 66.1 %all-gather.9.cloned.1.call-start = ((), (), s32[]{:S(2)}) async-start(), calls=%async_computation.8 | async-start | bytes 11059200 | tf_op jit(solution)/shard_map/all_gather | solution.py:189
  8.1 40.4 %copy-start.22 = (s32[128]{0:T(128)S(1)}, s32[128]{0:T(128)}, u32[]{:S(2)}) copy-start(s32[128]{0:T(128)} %param.19) | copy-start | bytes 1540
  8.1 100.2 %all-gather.11.cloned.1.call-start = ((), (), s32[]{:S(2)}) async-start(), calls=%async_computation.9 | async-start | bytes 3686400 | tf_op jit(solution)/shard_map/all_gather | solution.py:192
  8.8 175.7 %all-gather.13.cloned.1.call-start = ((), (), s32[]{:S(2)}) async-start(), calls=%async_computation.10 | async-start | bytes 14745600 | tf_op jit(solution)/shard_map/all_gather | solution.py:196
  9.6 251.1 %all-gather.15.cloned.1.call-start = ((), (), s32[]{:S(2)}) async-start(), calls=%async_computation.11 | async-start | bytes 14745600 | tf_op jit(solution)/shard_map/all_gather | solution.py:198
  10.1 429.0 %reduce-scatter.9.cloned.1.call-start = ((), (), s32[]{:S(2)}) async-start(), calls=%async_computation.12 | async-start | bytes 22118400 | tf_op jit(solution)/shard_map/reduce_scatter | solution.py:51
  260.6 14.4 %copy-start = (bf16[1280,5120]{1,0:T(8,128)(2,1)S(1)}, bf16[1280,5120]{1,0:T(8,128)(2,1)}, u32[]{:S(2)}) copy-start(bf16[1280,5120]{1,0:T(8,128)(2,1)} %all-gather.13.cloned.1.call-done) | copy-start | bytes 39321604
  283.2 5.8 copy-start.2
  309.4 295.7 %reduce-scatter.17.cloned.1.call-start = ((), (), s32[]{:S(2)}) async-start(), calls=%async_computation.17 | async-start | bytes 29491200 | tf_op jit(solution)/shard_map/reduce_scatter | solution.py:58
  326.0 445.1 %reduce-scatter.21.cloned.1.call-start = ((), (), s32[]{:S(2)}) async-start(), calls=%async_computation.20 | async-start | bytes 29491200 | tf_op jit(solution)/shard_map/reduce_scatter | solution.py:60
  342.9 494.8 %reduce-scatter.13.cloned.1.call-start = ((), (), s32[]{:S(2)}) async-start(), calls=%async_computation.15 | async-start | bytes 7372800 | tf_op jit(solution)/shard_map/reduce_scatter | solution.py:54
  346.8 524.0 %reduce-scatter.11.cloned.1.call-start = ((), (), s32[]{:S(2)}) async-start(), calls=%async_computation.13 | async-start | bytes 1536000 | tf_op jit(solution)/shard_map/reduce_scatter | solution.py:70
  442.0 466.6 %reduce-scatter.19.cloned.1.call-start = ((), (), s32[]{:S(2)}) async-start(), calls=%async_computation.18 | async-start | bytes 2048000 | tf_op jit(solution)/shard_map/reduce_scatter | solution.py:91
  608.4 338.6 %reduce-scatter.23.cloned.1.call-start = ((), (), s32[]{:S(2)}) async-start(), calls=%async_computation.21 | async-start | bytes 2048000 | tf_op jit(solution)/shard_map/reduce_scatter | solution.py:97
  774.4 172.6 %copy-start.9 = (bf16[20,64,128]{2,1,0:T(8,128)(2,1)S(1)}, bf16[20,64,128]{2,1,0:T(8,128)(2,1)}, u32[]{:S(2)}) copy-start(bf16[20,64,128]{2,1,0:T(8,128)(2,1)} %get-tuple-element.89) | copy-start | bytes 983044
  774.4 285.7 %reduce-scatter.15.cloned.1.call-start = ((), (), s32[]{:S(2)}) async-start(), calls=%async_computation.16 | async-start | bytes 512000 | tf_op jit(solution)/shard_map/reduce_scatter | solution.py:79
  839.6 240.1 %all-gather.17.cloned.1.call-start = ((), (), s32[]{:S(2)}) async-start(), calls=%async_computation.14 | async-start | bytes 1536000 | tf_op jit(solution)/shard_map/all_gather | solution.py:111
  870.8 211.8 %all-gather.19.cloned.1.call-start = ((), (), s32[]{:S(2)}) async-start(), calls=%async_computation.19 | async-start | bytes 2048000 | tf_op jit(solution)/shard_map/all_gather | solution.py:132
  908.6 177.9 %all-gather.21.cloned.1.call-start = ((), (), s32[]{:S(2)}) async-start(), calls=%async_computation.22 | async-start | bytes 2048000 | tf_op jit(solution)/shard_map/all_gather | solution.py:138
  (14 other events, 45.6 us)
Sparse Core Ops, SparseCore 0:
  10.0 63.3 all-gather.8
  75.3 32.8 all-gather.10
  110.1 74.3 all-gather.12
  186.2 74.3 all-gather.14
  309.5 129.6 reduce-scatter.8
  442.7 162.3 reduce-scatter.16
  608.8 162.3 reduce-scatter.20
  774.6 62.9 reduce-scatter.12
  840.6 30.0 reduce-scatter.10
  873.5 35.0 reduce-scatter.18
  911.6 35.3 reduce-scatter.22
  949.7 19.8 reduce-scatter.14
  971.2 30.5 all-gather.16
  1003.2 37.9 all-gather.18
  1042.8 43.7 all-gather.20
where the time goes:
time: 1100 us
  waiting for transfers between devices  781 us (71%)
  blocking collectives  139 us (13%)
  matrix products  110 us (10%)
  other arithmetic  36.9 us (3%)
  between operations  19.2 us (2%)
    reduce_scatter x1, waiting for transfers between devices, reduce_late(): lax.psum_scatter(values[9], 'fsdp', scatter_dimension=0, tiled=True)  163 us
    reduce_scatter x1, waiting for transfers between devices, reduce_late(): lax.psum_scatter(values[11], 'fsdp', scatter_dimension=0, tiled=True)  163 us
    reduce_scatter x1, waiting for transfers between devices, reduce_late(): lax.psum_scatter(values[2], 'fsdp', scatter_dimension=0, tiled=True)  92.3 us
    all_gather x1, waiting for transfers between devices, local(): lax.all_gather(w_up, 'fsdp', axis=0, tiled=True)  73.4 us
    unnamed x4, blocking collectives  71.4 us
    all_gather x1, waiting for transfers between devices, local(): lax.all_gather(w_down, 'fsdp', axis=0, tiled=True)  67.9 us
    reduce_scatter x1, waiting for transfers between devices, reduce_late(): lax.psum_scatter(values[5], 'fsdp', scatter_dimension=0, tiled=True)  63.1 us
    psum x1, blocking collectives, local(): lax.psum((jnp.sum(picked, axis=0), jnp.sum(picked * picked, axis=0)), ('d...  40.5 us
  transfers between devices with their start and end apart: 15, of which 12 were waited for; matrix products, arithmetic and copies ran while one was open for 9% of the time, Pallas kernels for 0%

commit v1 on v0

--- a/solution.py
+++ b/solution.py
@@ -9,6 +9,17 @@
 HEAD_DIM = 64
 CELLS_DEV = 2
 EPS = 1e-05
+
+
+def gather_around(x, axis, dim):
+    ways = lax.axis_size(axis)
+    pieces = [x]
+    for far in range(1, ways):
+        pieces.append(
+            lax.ppermute(pieces[far - 1], axis, [(d, (d - 1) % ways) for d in range(ways)])
+        )
+    line = jnp.concatenate(pieces, axis=dim)
+    return jnp.roll(line, lax.axis_index(axis) * x.shape[dim], axis=dim)
 
 
 def norm_forward(values, norm_gain, norm_bias):
@@ -189,7 +200,7 @@
         lax.all_gather(w_qkv, "fsdp", axis=0, tiled=True),
         lax.all_gather(b_query, "fsdp", axis=0, tiled=True),
         lax.all_gather(b_value, "fsdp", axis=0, tiled=True),
-        lax.all_gather(w_out, "fsdp", axis=0, tiled=True),
+        gather_around(w_out, "fsdp", 0),
         lax.all_gather(b_out, "fsdp", axis=0, tiled=True),
         lax.all_gather(ln2_gain, "fsdp", axis=0, tiled=True),
         lax.all_gather(ln2_bias, "fsdp", axis=0, tiled=True),

time: 1100 us -> 1100 us (level)
  waiting for transfers between devices: 781 us -> 736 us
  starting transfers between devices: 0.6 us -> 19.6 us
  local copies, waits for them, and re-layouts: 10.8 us -> 23 us
    all_gather x1, waiting for transfers between devices: 73.4 us -> 21.7 us  [local(): lax.all_gather(w_up, 'fsdp', axis=0, tiled=True)]
    ppermute x0 -> x7, waiting for transfers between devices: none -> 46.7 us  [gather_around(): lax.ppermute(pieces[far - 1], axis, [(d, (d - 1) % ways) for d in range(w...]
    all_gather x1, waiting for transfers between devices: 24.9 us -> 0.01 us  [local(): lax.all_gather(w_qkv, 'fsdp', axis=0, tiled=True)]
    ppermute x0 -> x7, starting transfers between devices: none -> 19 us  [gather_around(): lax.ppermute(pieces[far - 1], axis, [(d, (d - 1) % ways) for d in range(w...]
    all_gather x1, waiting for transfers between devices: 26.8 us -> 12 us  [local(): lax.all_gather(w_out, 'fsdp', axis=0, tiled=True)]
    unnamed x100 -> x119, local copies, waits for them, and re-layouts: 8.09 us -> 19.6 us
  transfers between devices with their start and end apart: 15 -> 22, of which waited for: 12 -> 17; matrix products, arithmetic and copies ran while one was open for 9% -> 13% of each run, Pallas kernels for 0% -> 0%
where the time goes in v1:
time: 1100 us; the launch traced here: 1090 us
  waiting for transfers between devices  736 us (67%)
  blocking collectives  143 us (13%)
  matrix products  110 us (10%)
  other arithmetic  37 us (3%)
  local copies, waits for them, and re-layouts  23 us (2%)
  starting transfers between devices  19.6 us (2%)
  between operations  19.3 us (2%)
    reduce_scatter x1, waiting for transfers between devices, reduce_late(): lax.psum_scatter(values[9], 'fsdp', scatter_dimension=0, tiled=True)  163 us
    reduce_scatter x1, waiting for transfers between devices, reduce_late(): lax.psum_scatter(values[11], 'fsdp', scatter_dimension=0, tiled=True)  163 us
    reduce_scatter x1, waiting for transfers between devices, reduce_late(): lax.psum_scatter(values[2], 'fsdp', scatter_dimension=0, tiled=True)  92.4 us
    unnamed x4, blocking collectives  76.5 us
    all_gather x1, waiting for transfers between devices, local(): lax.all_gather(w_down, 'fsdp', axis=0, tiled=True)  68.1 us
    reduce_scatter x1, waiting for transfers between devices, reduce_late(): lax.psum_scatter(values[5], 'fsdp', scatter_dimension=0, tiled=True)  63.1 us
    ppermute x7, waiting for transfers between devices, gather_around(): lax.ppermute(pieces[far - 1], axis, [(d, (d - 1) % ways) for d in range(w...  46.7 us
    psum x1, blocking collectives, local(): lax.psum((jnp.sum(picked, axis=0), jnp.sum(picked * picked, axis=0)), ('d...  40.4 us
  transfers between devices with their start and end apart: 22, of which 17 were waited for; matrix products, arithmetic and copies ran while one was open for 13% of the time, Pallas kernels for 0%

profile of v1, /device:TPU:0, one launch (start us, length us, event | category | flops | bytes accessed | tf_op | source)
XLA Modules:
  0.0 1088.4 jit_solution(6493740700763325038)
XLA Ops:
  24.7 31.0 %all-reduce.37 = (bf16[1280]{0:T(1024)(128)(2,1)S(1)}, bf16[1280]{0:T(1024)(128)(2,1)S(1)}, bf16[1280]{0:T(1024)(128)(2,1)S(1)}, bf16[1280]{0:T(1024)(128)(2,1)S...) all-reduce(bf16[1280]{0:T(1024)(128)(2,1)S(1)} %dynamic-update-slic, ...), channel_id=1, replica_groups=mesh['dp'=4,'fsdp'=8] {'fsdp'}, use_global_device_ids=true, to_apply=%add.1 | all-reduce | flops 10240 | bytes 40960
  65.6 12.6 %collective-permute-done.2 = bf16[160,1280]{1,0:T(8,128)(2,1)S(1)} collective-permute-done((bf16[160,1280]{1,0:T(8,128)(2,1)S(1)}, bf16[160,1280]{1,0:T(8,128)(2,1)S(1)}, u32[]{:S(2)}, u32[]{:S(2)}) %collective-permute-start.2) | collective-permute-done | bytes 409632 | tf_op jit(solution)/shard_map/ppermute | solution.py:19
  103.3 12.7 %collective-permute-done.5 = bf16[160,1280]{1,0:T(8,128)(2,1)S(1)} collective-permute-done((bf16[160,1280]{1,0:T(8,128)(2,1)S(1)}, bf16[160,1280]{1,0:T(8,128)(2,1)S(1)}, u32[]{:S(2)}, u32[]{:S(2)}) %collective-permute-start.5) | collective-permute-done | bytes 409632 | tf_op jit(solution)/shard_map/ppermute | solution.py:19
  142.4 21.7 %all-gather.11.cloned.1.call-done = bf16[1280,5120]{1,0:T(8,128)(2,1)} async-done(((bf16[160,5120]{1,0:T(8,128)(2,1)}), bf16[1280,5120]{1,0:T(8,128)(2,1)}) %all-gather.11.cloned.1.call-update) | async-done | bytes 13107216 | tf_op jit(solution)/shard_map/all_gather | solution.py:207
  164.2 8.2 convolution_add_fusion
  172.4 68.1 %all-gather.13.cloned.1.call-done = bf16[5120,1280]{1,0:T(8,128)(2,1)} async-done(((bf16[640,1280]{1,0:T(8,128)(2,1)}), bf16[5120,1280]{1,0:T(8,128)(2,1)}) %all-gather.13.cloned.1.call-update) | async-done | bytes 13107216 | tf_op jit(solution)/shard_map/all_gather | solution.py:209
  240.5 14.4 %convert_reduce_fusion = (f32[5120]{0:T(1024)S(1)}, bf16[128,5120]{1,0:T(8,128)(2,1)}, f32[128,5120]{1,0:T(8,128)}) fusion(f32[128,5120]{1,0:T(8,128)} %convolution_add_fusion, bf16[128,1280]{1,0:T(8,128)(2,1)} %param.33, bf16[5120,1280]{1,0:T(8,128)(2,1)} %all-gather.13.cloned.1.call-done), kind=kOutput, calls=%fused_computation.6 | convolution fusion | flops 1726213120 | bytes 20008960 | tf_op jit(solution)/shard_map/td,fd->tf/dot_general | solution.py:286
  263.1 12.0 %all-gather.15.cloned.1.call-done = bf16[1280,1280]{1,0:T(8,128)(2,1)} async-done(((bf16[160,1280]{1,0:T(8,128)(2,1)}), bf16[1280,1280]{1,0:T(8,128)(2,1)}) %all-gather.15.cloned.1.call-update) | async-done | bytes 3276816 | tf_op jit(solution)/shard_map/all_gather | solution.py:274
  291.7 9.4 fusion.57
  302.4 15.4 %fusion.76 = f32[1280,5120]{1,0:T(8,128)} fusion(bf16[128,5120]{1,0:T(8,128)(2,1)S(1)} %copy-done.4, f32[128,1280]{1,0:T(8,128)S(1)} %get-tuple-element.82, f32[1280]{0:T(1024)S(1)} %convert_element_type.233, f32[1280]{0:T(1024)S(1)} %convert_element_type.232, f32[128]{0:T(128)S(1)} %add_rsqrt_fusion, f32[128]{0:T(128)S(1)} %broadcast_multiply_fusion.5), kind=kOutput, calls=%fused_computation.140 | convolution fusion | flops 1678540800 | bytes 28191744 | tf_op jit(solution)/shard_map/td,tf->df/dot_general | solution.py:289
  321.9 12.7 %fusion.85 = f32[5120,1280]{1,0:T(8,128)} fusion(bf16[128,5120]{1,0:T(8,128)(2,1)S(1)} %multiply_convert_fusion, bf16[128,1280]{1,0:T(8,128)(2,1)S(1)} %copy-done.10), kind=kOutput, calls=%fused_computation.146 | convolution fusion | flops 1677721600 | bytes 27852800 | tf_op jit(solution)/shard_map/tf,td->fd/dot_general | solution.py:285
  338.6 92.4 %reduce-scatter.9.cloned.1.call-done = f32[160,3840]{1,0:T(8,128)} async-done(((f32[1280,3840]{1,0:T(8,128)}), f32[160,3840]{1,0:T(8,128)}) %reduce-scatter.9.cloned.1.call-update) | async-done | bytes 2457616 | tf_op jit(solution)/shard_map/reduce_scatter | solution.py:62
  433.9 163.0 %reduce-scatter.17.cloned.1.call-done = f32[160,5120]{1,0:T(8,128)} async-done(((f32[1280,5120]{1,0:T(8,128)}), f32[160,5120]{1,0:T(8,128)}) %reduce-scatter.17.cloned.1.call-update) | async-done | bytes 3276816 | tf_op jit(solution)/shard_map/reduce_scatter | solution.py:69
  600.2 162.7 %reduce-scatter.21.cloned.1.call-done = f32[640,1280]{1,0:T(8,128)} async-done(((f32[5120,1280]{1,0:T(8,128)}), f32[640,1280]{1,0:T(8,128)}) %reduce-scatter.21.cloned.1.call-update) | async-done | bytes 3276816 | tf_op jit(solution)/shard_map/reduce_scatter | solution.py:71
  766.3 63.1 %reduce-scatter.13.cloned.1.call-done = f32[160,1280]{1,0:T(8,128)} async-done(((f32[1280,1280]{1,0:T(8,128)}), f32[160,1280]{1,0:T(8,128)}) %reduce-scatter.13.cloned.1.call-update) | async-done | bytes 819216 | tf_op jit(solution)/shard_map/reduce_scatter | solution.py:65
  831.4 31.1 %reduce-scatter.11.cloned.1.call-done = bf16[40,3840]{1,0:T(8,128)(2,1)} async-done(((bf16[160,3840]{1,0:T(8,128)(2,1)}), bf16[40,3840]{1,0:T(8,128)(2,1)}) %reduce-scatter.11.cloned.1.call-update) | async-done | bytes 307216 | tf_op jit(solution)/shard_map/reduce_scatter | solution.py:81
  862.6 37.7 %reduce-scatter.19.cloned.1.call-done = bf16[40,5120]{1,0:T(8,128)(2,1)} async-done(((bf16[160,5120]{1,0:T(8,128)(2,1)}), bf16[40,5120]{1,0:T(8,128)(2,1)}) %reduce-scatter.19.cloned.1.call-update) | async-done | bytes 409616 | tf_op jit(solution)/shard_map/reduce_scatter | solution.py:102
  904.3 34.4 %reduce-scatter.23.cloned.1.call-done = bf16[160,1280]{1,0:T(8,128)(2,1)} async-done(((bf16[640,1280]{1,0:T(8,128)(2,1)}), bf16[160,1280]{1,0:T(8,128)(2,1)}) %reduce-scatter.23.cloned.1.call-update) | async-done | bytes 409616 | tf_op jit(solution)/shard_map/reduce_scatter | solution.py:108
  938.8 8.2 fusion.47
  947.2 25.2 %all-reduce.36 = (bf16[1280]{0:T(1024)(128)(2,1)S(1)}, bf16[1280]{0:T(1024)(128)(2,1)S(1)}, bf16[1280]{0:T(1024)(128)(2,1)S(1)}, bf16[1280]{0:T(1024)(128)(2,1)S...) all-reduce(f32[1280]{0:T(1024)S(1)} %get-tuple-element.19, ...), channel_id=2, replica_groups=mesh['dp'=4,'fsdp'=8] {'fsdp'}, use_global_device_ids=true, to_apply=%region_15.16.clone | all-reduce | flops 15360 | bytes 92160
  973.0 10.7 all-reduce.39
  986.4 9.6 all-reduce.38
  1008.7 40.4 %all-reduce.35 = (f32[1280]{0:T(1024)S(1)}, f32[1280]{0:T(1024)S(1)}) all-reduce(f32[1280]{0:T(1024)S(1)} %get-tuple-element.24, f32[1280]{0:T(1024)S(1)} %get-tuple-element.23), channel_id=1, replica_groups=mesh['dp'=4,'fsdp'=8] {'dp','fsdp'}, use_global_device_ids=true, to_apply=%region_50.51 | all-reduce | flops 2560 | bytes 20480 | tf_op jit(solution)/shard_map/psum | solution.py:248
  1051.9 18.6 %all_gather.101 = bf16[160,1280]{1,0:T(8,128)(2,1)S(1)} all-gather(bf16[40,1280]{1,0:T(8,128)(2,1)} %reduce-scatter.15.cloned.1.call-done), channel_id=1, replica_groups=mesh['dp'=4,'fsdp'=8] {'dp'}, dimensions={0}, use_global_device_ids=true | all-gather | bytes 512000 | tf_op jit(solution)/shard_map/all_gather | solution.py:131
  (237 shorter events, 153.8 us)
Async XLA Ops:
  7.3 124.0 %all-gather.9.cloned.1.call-start = ((), (), s32[]{:S(2)}) async-start(), calls=%async_computation.8 | async-start | bytes 11059200 | tf_op jit(solution)/shard_map/all_gather | solution.py:200
  8.1 72.9 %copy-start.6 = (bf16[160,1280]{1,0:T(8,128)(2,1)S(1)}, bf16[160,1280]{1,0:T(8,128)(2,1)}, u32[]{:S(2)}) copy-start(bf16[160,1280]{1,0:T(8,128)(2,1)} %param.25) | copy-start | bytes 1228804
  8.1 156.1 %all-gather.11.cloned.1.call-start = ((), (), s32[]{:S(2)}) async-start(), calls=%async_computation.9 | async-start | bytes 14745600 | tf_op jit(solution)/shard_map/all_gather | solution.py:207
  8.8 231.6 %all-gather.13.cloned.1.call-start = ((), (), s32[]{:S(2)}) async-start(), calls=%async_computation.10 | async-start | bytes 14745600 | tf_op jit(solution)/shard_map/all_gather | solution.py:209
  9.6 265.5 %all-gather.15.cloned.1.call-start = ((), (), s32[]{:S(2)}) async-start(), calls=%async_computation.11 | async-start | bytes 3686400 | tf_op jit(solution)/shard_map/all_gather | solution.py:274
  9.6 8.9 collective-permute-start
  13.0 417.9 %reduce-scatter.9.cloned.1.call-start = ((), (), s32[]{:S(2)}) async-start(), calls=%async_computation.12 | async-start | bytes 22118400 | tf_op jit(solution)/shard_map/reduce_scatter | solution.py:62
  18.5 45.5 %collective-permute-start.1 = (bf16[160,1280]{1,0:T(8,128)(2,1)S(1)}, bf16[160,1280]{1,0:T(8,128)(2,1)S(1)}, u32[]{:S(2)}, u32[]{:S(2)}) collective-permute-start(bf16[160,1280]{1,0:T(8,128)(2,1)S(1)} %collective-permute-done), channel_id=1, source_target_pairs={{0,7},{1,0},{2,1},{3,2},{4,3},{5,4},{6,5},{7,6},{8,15},{9,8},{10,9... | collective-permute-start | bytes 1228808 | tf_op jit(solution)/shard_map/ppermute | solution.py:19
  64.0 14.1 %collective-permute-start.2 = (bf16[160,1280]{1,0:T(8,128)(2,1)S(1)}, bf16[160,1280]{1,0:T(8,128)(2,1)S(1)}, u32[]{:S(2)}, u32[]{:S(2)}) collective-permute-start(bf16[160,1280]{1,0:T(8,128)(2,1)S(1)} %collective-permute-done.1), channel_id=1, source_target_pairs={{0,7},{1,0},{2,1},{3,2},{4,3},{5,4},{6,5},{7,6},{8,15},{9,8},{10,9... | collective-permute-start | bytes 1228808 | tf_op jit(solution)/shard_map/ppermute | solution.py:19
  78.2 8.3 collective-permute-start.3
  86.5 12.4 %collective-permute-start.4 = (bf16[160,1280]{1,0:T(8,128)(2,1)S(1)}, bf16[160,1280]{1,0:T(8,128)(2,1)S(1)}, u32[]{:S(2)}, u32[]{:S(2)}) collective-permute-start(bf16[160,1280]{1,0:T(8,128)(2,1)S(1)} %collective-permute-done.3), channel_id=1, source_target_pairs={{0,7},{1,0},{2,1},{3,2},{4,3},{5,4},{6,5},{7,6},{8,15},{9,8},{10,9... | collective-permute-start | bytes 1228808 | tf_op jit(solution)/shard_map/ppermute | solution.py:19
  98.9 17.1 %collective-permute-start.5 = (bf16[160,1280]{1,0:T(8,128)(2,1)S(1)}, bf16[160,1280]{1,0:T(8,128)(2,1)S(1)}, u32[]{:S(2)}, u32[]{:S(2)}) collective-permute-start(bf16[160,1280]{1,0:T(8,128)(2,1)S(1)} %collective-permute-done.4), channel_id=1, source_target_pairs={{0,7},{1,0},{2,1},{3,2},{4,3},{5,4},{6,5},{7,6},{8,15},{9,8},{10,9... | collective-permute-start | bytes 1228808 | tf_op jit(solution)/shard_map/ppermute | solution.py:19
  116.0 8.3 collective-permute-start.6
  301.1 295.7 %reduce-scatter.17.cloned.1.call-start = ((), (), s32[]{:S(2)}) async-start(), calls=%async_computation.17 | async-start | bytes 29491200 | tf_op jit(solution)/shard_map/reduce_scatter | solution.py:69
  317.8 445.1 %reduce-scatter.21.cloned.1.call-start = ((), (), s32[]{:S(2)}) async-start(), calls=%async_computation.20 | async-start | bytes 29491200 | tf_op jit(solution)/shard_map/reduce_scatter | solution.py:71
  334.6 494.8 %reduce-scatter.13.cloned.1.call-start = ((), (), s32[]{:S(2)}) async-start(), calls=%async_computation.15 | async-start | bytes 7372800 | tf_op jit(solution)/shard_map/reduce_scatter | solution.py:65
  338.5 524.0 %reduce-scatter.11.cloned.1.call-start = ((), (), s32[]{:S(2)}) async-start(), calls=%async_computation.13 | async-start | bytes 1536000 | tf_op jit(solution)/shard_map/reduce_scatter | solution.py:81
  433.8 466.6 %reduce-scatter.19.cloned.1.call-start = ((), (), s32[]{:S(2)}) async-start(), calls=%async_computation.18 | async-start | bytes 2048000 | tf_op jit(solution)/shard_map/reduce_scatter | solution.py:102
  600.2 338.6 %reduce-scatter.23.cloned.1.call-start = ((), (), s32[]{:S(2)}) async-start(), calls=%async_computation.21 | async-start | bytes 2048000 | tf_op jit(solution)/shard_map/reduce_scatter | solution.py:108
  766.2 172.6 %copy-start.11 = (bf16[20,64,128]{2,1,0:T(8,128)(2,1)S(1)}, bf16[20,64,128]{2,1,0:T(8,128)(2,1)}, u32[]{:S(2)}) copy-start(bf16[20,64,128]{2,1,0:T(8,128)(2,1)} %get-tuple-element.89) | copy-start | bytes 983044
  766.2 285.7 %reduce-scatter.15.cloned.1.call-start = ((), (), s32[]{:S(2)}) async-start(), calls=%async_computation.16 | async-start | bytes 512000 | tf_op jit(solution)/shard_map/reduce_scatter | solution.py:90
  831.4 240.0 %all-gather.17.cloned.1.call-start = ((), (), s32[]{:S(2)}) async-start(), calls=%async_computation.14 | async-start | bytes 1536000 | tf_op jit(solution)/shard_map/all_gather | solution.py:122
  862.6 211.7 %all-gather.19.cloned.1.call-start = ((), (), s32[]{:S(2)}) async-start(), calls=%async_computation.19 | async-start | bytes 2048000 | tf_op jit(solution)/shard_map/all_gather | solution.py:143
  900.4 177.8 %all-gather.21.cloned.1.call-start = ((), (), s32[]{:S(2)}) async-start(), calls=%async_computation.22 | async-start | bytes 2048000 | tf_op jit(solution)/shard_map/all_gather | solution.py:149
  (23 other events, 321.0 us)
Sparse Core Ops, SparseCore 0:
  10.1 71.7 all-gather.8
  83.7 80.3 all-gather.10
  166.1 74.3 all-gather.12
  242.2 32.8 all-gather.14
  301.2 129.6 reduce-scatter.8
  434.5 162.3 reduce-scatter.16
  600.6 162.3 reduce-scatter.20
  766.4 62.9 reduce-scatter.12
  832.4 30.0 reduce-scatter.10
  865.3 35.0 reduce-scatter.18
  903.4 35.3 reduce-scatter.22
  941.5 19.7 reduce-scatter.14
  962.9 30.5 all-gather.16
  995.0 37.9 all-gather.18
  1034.5 43.6 all-gather.20
